TPU v7x, 512 devices: a whole 4x8x8 slice. The times are simulated.
512 devices in a mesh: dp: 8 (over y), expert: 64 (over z, x, core).
Axes of the slice: x: 4, y: 8, z: 8, core: 2. Of those that a mesh axis runs over, the one named last changes fastest.
Arguments:
- tokens: bfloat16 [4096, 4096], P('expert', 'dp'), may hold values from -6 to 6
- expert_ids: int32 [4096, 8], P('expert'), may hold values from 0 to 63, all different within a row; in each aligned block of 64 rows (0 to 63, 64 to 127, ...) at most 16 rows name the same one
- gate_weights: float32 [4096, 8], P('expert'), may hold values from 0.05 to 1
- gate_proj: bfloat16 [64, 4096, 1536], P('expert', 'dp'), may hold values from -0.09375 to 0.09375
- up_proj: bfloat16 [64, 4096, 1536], P('expert', 'dp'), may hold values from -0.09375 to 0.09375
- down_proj: bfloat16 [64, 1536, 4096], P('expert', None, 'dp'), may hold values from -0.15625 to 0.15625
Outputs:
- combined: bfloat16 [4096, 4096], P('expert', 'dp')
Inputs may be any that keep to these rules, and one draw needn't show every extreme that they name: `expert_ids`: each row names 8 different experts. Among the 64 rows of one device (one aligned block), no expert is named by more than 16 rows, and in every draw some expert is named by exactly 16 rows of some block.
All inputs are finite; a program needn't handle non-finite values.
Results may differ from a plain program's by a relative error of at most 0.029.
Values may be sent and summed in bfloat16 or wider, within the bound.
A program may use at most 64 MiB of HBM per device.

v0:
```python
import jax
import jax.numpy as jnp
from jax import lax
from jax.sharding import PartitionSpec as P


def block_places(block_ids, expert_count, capacity):
    tok_count, top_count = block_ids.shape
    flat_ids = block_ids.reshape(tok_count * top_count)
    matches = (flat_ids[:, None] == jnp.arange(expert_count, dtype=jnp.int32)[None, :]).astype(
        jnp.int32
    )
    earlier = jnp.cumsum(matches, axis=0) - matches
    slot_index = jnp.sum(earlier * matches, axis=1)
    return (flat_ids * capacity + slot_index).reshape(tok_count, top_count)


def body(tokens, expert_ids, gate_weights, gate_proj, up_proj, down_proj):
    tok_count, top_count = expert_ids.shape
    row_width = tokens.shape[1]
    sources = lax.axis_size("expert")
    capacity = 2 * tok_count * top_count // sources
    positions = jnp.arange(sources * capacity, dtype=jnp.int32)
    places = block_places(expert_ids, sources, capacity)
    matches = places[:, :, None] == positions[None, None, :]
    weighting = jnp.sum(jnp.where(matches, gate_weights[:, :, None], 0.0), axis=1)
    chosen = jnp.any(matches, axis=1).astype(jnp.bfloat16)
    outgoing = lax.dot_general(
        chosen, tokens, (((0,), (0,)), ((), ())), preferred_element_type=jnp.float32
    ).astype(jnp.bfloat16)
    incoming = lax.all_to_all(
        outgoing.reshape(sources, capacity, row_width),
        "expert",
        split_axis=0,
        concat_axis=0,
        tiled=True,
    )
    expert_rows = incoming.reshape(sources * capacity, row_width)
    gate_part = jnp.dot(expert_rows, gate_proj[0], preferred_element_type=jnp.float32)
    up_part = jnp.dot(expert_rows, up_proj[0], preferred_element_type=jnp.float32)
    gate_sum, up_sum = (
        lax.psum(gate_part.astype(jnp.bfloat16), "dp").astype(jnp.float32),
        lax.psum(up_part.astype(jnp.bfloat16), "dp").astype(jnp.float32),
    )
    hidden = (jax.nn.silu(gate_sum) * up_sum).astype(jnp.bfloat16)
    expert_out = jnp.dot(hidden, down_proj[0], preferred_element_type=jnp.float32).astype(
        jnp.bfloat16
    )
    returned = lax.all_to_all(
        expert_out.reshape(sources, capacity, row_width),
        "expert",
        split_axis=0,
        concat_axis=0,
        tiled=True,
    )
    returned_flat = returned.reshape(sources * capacity, row_width)
    weight_high = weighting.astype(jnp.bfloat16)
    weight_low = (weighting - weight_high.astype(jnp.float32)).astype(jnp.bfloat16)
    combined = jnp.dot(weight_high, returned_flat, preferred_element_type=jnp.float32)
    combined = combined + jnp.dot(weight_low, returned_flat, preferred_element_type=jnp.float32)
    return combined.astype(jnp.bfloat16)


def solution(mesh):
    placed = (
        P("expert", "dp"),
        P("expert", None),
        P("expert", None),
        P("expert", "dp", None),
        P("expert", "dp", None),
        P("expert", None, "dp"),
    )
    return jax.shard_map(
        body, mesh=mesh, in_specs=placed, out_specs=P("expert", "dp"), check_vma=False
    )
```

profile of v0, /device:TPU:1, one launch (start us, length us, event | category | flops | bytes accessed | tf_op | source)
XLA Modules:
  0.0 266.4 jit_solution(7959144195242189206)
XLA Ops:
  6.5 0.0 copy-start
  6.5 0.0 all-reduce.3.cloned.1.call-start
  6.5 0.9 copy.21
  7.4 0.1 eq.42
  7.5 0.1 eq.38
  7.6 1.2 reduce-window.6
  8.8 0.2 slice_reduce_fusion
  9.1 0.1 fusion.19
  9.2 0.1 reduce_sum.21
  9.3 0.1 copy.24
  9.4 0.7 multiply_add_fusion
  10.1 0.1 copy.25
  10.2 0.7 fusion.7
  10.9 1.3 convolution_convert_fusion.2
  12.2 42.6 %all_to_all.10 = bf16[64,16,512]{2,1,0:T(8,128)(2,1)S(1)} all-to-all(bf16[64,16,512]{2,1,0:T(8,128)(2,1)S(1)} %bitcast.42), channel_id=1, replica_groups=mesh['dp'=8,'expert'=64] {'expert'}, dimensions={0} | all-to-all | bytes 2097152 | tf_op jit(solution)/shard_map/all_to_all | solution.py:31
  54.8 0.0 copy-done
  54.8 0.0 copy-start.2
  54.8 3.5 %convolution_convert_fusion = bf16[1024,1536]{1,0:T(8,128)(2,1)} fusion(bf16[1024,512]{1,0:T(8,128)(2,1)S(1)} %bitcast.44, bf16[1,512,1536]{2,1,0:T(8,128)(2,1)S(1)} %copy-done), kind=kOutput, calls=%fused_computation.7 | convolution fusion | flops 1612185600 | bytes 5767168 | tf_op jit(solution)/shard_map/dot_general | solution.py:40
  58.3 0.0 copy-done.2
  58.3 3.4 %convolution_convert_fusion.1 = bf16[1024,1536]{1,0:T(8,128)(2,1)} fusion(bf16[1024,512]{1,0:T(8,128)(2,1)S(1)} %bitcast.45, bf16[1,512,1536]{2,1,0:T(8,128)(2,1)S(1)} %copy-done.2), kind=kOutput, calls=%fused_computation.8 | convolution fusion | flops 1612185600 | bytes 5767168 | tf_op jit(solution)/shard_map/dot_general | solution.py:39
  61.8 0.0 all-reduce.3.cloned.1.call-update
  61.8 151.3 %all-reduce.3.cloned.1.call-done = (bf16[1024,1536]{1,0:T(8,128)(2,1)}, bf16[1024,1536]{1,0:T(8,128)(2,1)}) async-done(((bf16[1024,1536]{1,0:T(8,128)(2,1)}, bf16[1024,1536]{1,0:T(8,128)(2,1)}), (bf16[1024,1536]{1,0:T(8,128)(2,1)}, bf16[1024,1536]{1,0:T(8,128)(2,1)})) %all-reduce.3.cloned.1.call-update) | async-done | bytes 6291472 | tf_op jit(solution)/shard_map/psum | solution.py:43
  213.1 0.0 copy-start.1
  213.1 6.2 %fusion.11 = bf16[1024,512]{1,0:T(8,128)(2,1)} fusion(bf16[1,1536,512]{2,1,0:T(8,128)(2,1)} %param.11, bf16[1024,1536]{1,0:T(8,128)(2,1)} %get-tuple-element.5, bf16[1024,1536]{1,0:T(8,128)(2,1)} %get-tuple-element.6), kind=kOutput, calls=%fused_computation.16 | convolution fusion | flops 1623719936 | bytes 8912896 | tf_op jit(solution)/shard_map/dot_general | solution.py:46
  219.3 11.0 %all-to-all-start.1 = ((bf16[64,16,512]{2,1,0:T(8,128)(2,1)}), bf16[64,16,512]{2,1,0:T(8,128)(2,1)S(1)}, u32[]{:S(2)}, u32[]{:S(2)}) async-start(bf16[64,16,512]{2,1,0:T(8,128)(2,1)} %bitcast.43), calls=%async_computation.1 | async-start | bytes 2097152 | tf_op jit(solution)/shard_map/all_to_all | solution.py:49
  230.4 0.0 copy-done.1
  230.4 0.1 copy.26
  230.5 0.7 select_reduce_fusion
  231.2 27.2 %all-to-all-done.1 = bf16[64,16,512]{2,1,0:T(8,128)(2,1)S(1)} async-done(((bf16[64,16,512]{2,1,0:T(8,128)(2,1)}), bf16[64,16,512]{2,1,0:T(8,128)(2,1)S(1)}, u32[]{:S(2)}, u32[]{:S(2)}) %all-to-all-start.1) | async-done | bytes 1048608 | tf_op jit(solution)/shard_map/all_to_all | solution.py:49
  258.3 0.3 fusion.22
  258.6 0.9 fusion.16
  (3 shorter events, 0.1 us)
Async XLA Ops:
  6.5 48.3 %copy-start = (bf16[1,512,1536]{2,1,0:T(8,128)(2,1)S(1)}, bf16[1,512,1536]{2,1,0:T(8,128)(2,1)}, u32[]{:S(2)}) copy-start(bf16[1,512,1536]{2,1,0:T(8,128)(2,1)} %param.10) | copy-start | bytes 4718596
  6.5 206.6 %all-reduce.3.cloned.1.call-start = ((), (), s32[]{:S(2)}) async-start(), calls=%async_computation.2 | async-start | bytes 12582912 | tf_op jit(solution)/shard_map/psum | solution.py:43
  54.8 3.5 %copy-start.2 = (bf16[1,512,1536]{2,1,0:T(8,128)(2,1)S(1)}, bf16[1,512,1536]{2,1,0:T(8,128)(2,1)}, u32[]{:S(2)}) copy-start(bf16[1,512,1536]{2,1,0:T(8,128)(2,1)} %param.9) | copy-start | bytes 4718596
  213.1 17.3 %copy-start.1 = (f32[64,8]{0,1:T(8,128)S(1)}, f32[64,8]{0,1:T(8,128)}, u32[]{:S(2)}) copy-start(f32[64,8]{0,1:T(8,128)} %param.8) | copy-start | bytes 6148
  219.3 39.0 %all-to-all-start.1 = ((bf16[64,16,512]{2,1,0:T(8,128)(2,1)}), bf16[64,16,512]{2,1,0:T(8,128)(2,1)S(1)}, u32[]{:S(2)}, u32[]{:S(2)}) async-start(bf16[64,16,512]{2,1,0:T(8,128)(2,1)} %bitcast.43), calls=%async_computation.1 | async-start | bytes 2097152 | tf_op jit(solution)/shard_map/all_to_all | solution.py:49
Sparse Core Ops, SparseCore 0:
  61.9 151.1 all-reduce.2
where the time goes:
time: 267 us; the launch traced here: 266 us
  waiting for transfers between devices  178 us (67%)
  blocking collectives  42.6 us (16%)
  matrix products  15.7 us (6%)
  between operations  13.5 us (5%)
  starting transfers between devices  11 us (4%)
  other arithmetic  3.49 us (1%)
    psum x1, waiting for transfers between devices, body(): lax.psum(up_part.astype(jnp.bfloat16), 'dp').astype(jnp.float32)  151 us
    all_to_all x1, blocking collectives, body(): lax.all_to_all(outgoing.reshape(sources, capacity, row_width), 'expert',...  42.6 us
    all_to_all x1, waiting for transfers between devices, body(): lax.all_to_all(expert_out.reshape(sources, capacity, row_width), 'expert'...  27.2 us
    all_to_all x1, starting transfers between devices, body(): lax.all_to_all(expert_out.reshape(sources, capacity, row_width), 'expert'...  11 us
    dot_general x1, matrix products, body(): jnp.dot(hidden, down_proj[0], preferred_element_type=jnp.float32)  6.23 us
  transfers between devices with their start and end apart: 2, of which 2 were waited for; matrix products, arithmetic and copies ran while one was open for 0% of the time, Pallas kernels for 0%

commit v1 on v0

v1 whole, which is shorter than its diff:
```python
import functools

import jax
import jax.numpy as jnp
from jax import lax
from jax.experimental import pallas as pl
from jax.experimental.pallas import tpu as pltpu
from jax.sharding import PartitionSpec as P

MESH = pl.DeviceIdType.MESH
F32 = jnp.float32
BF16 = jnp.bfloat16


def quotient(a, b):
    return a // b if isinstance(a, int) else lax.div(a, jnp.int32(b))


def residue(a, b):
    return a % b if isinstance(a, int) else lax.rem(a, jnp.int32(b))


def iota(shape, dim):
    return lax.broadcasted_iota(jnp.int32, shape, dim)


def layer(
    n, per, ids_hbm, gw_hbm, tok_hbm, gate_hbm, up_hbm, down_hbm, out_ref,
    ids_ref, gw_ref, tok_ref, w_buf, d_buf, code_ref, mix_ref, packed, rows, rs_out, rs_in, hid, outs, ret,
    load_sem, pack_send, pack_recv, rs_send, rs_recv, ag_send, ag_recv, ret_send, ret_recv,
):
    y = lax.axis_index("dp")
    me = lax.axis_index("expert")
    z, r = quotient(me, per), residue(me, per)
    x, c = quotient(r, 2), residue(r, 2)
    n_x, half, mid = per // 2, per // 2, n // 2
    experts = n * per
    top, toks = ids_ref.shape
    width = tok_ref.shape[1]
    cap = packed.shape[2]
    m_rows = half * cap
    ff = w_buf.shape[2]
    tile = min(ff, 512)
    sub_rows = m_rows // 2
    ahead, behind = residue(y + 1, n), residue(y + n - 1, n)
    steps = n - 1

    small = [
        pltpu.make_async_copy(ids_hbm, ids_ref, load_sem.at[3]),
        pltpu.make_async_copy(gw_hbm, gw_ref, load_sem.at[4]),
        pltpu.make_async_copy(tok_hbm, tok_ref, load_sem.at[5]),
    ]
    loads = [
        pltpu.make_async_copy(gate_hbm, w_buf.at[0], load_sem.at[0]),
        pltpu.make_async_copy(up_hbm, w_buf.at[1], load_sem.at[1]),
        pltpu.make_async_copy(down_hbm, d_buf, load_sem.at[2]),
    ]
    for load in small + loads:
        load.start()
    barrier = pltpu.get_barrier_semaphore()

    def greet(i, carry):
        pl.semaphore_signal(
            barrier, inc=1, device_id={"expert": residue(me + i, experts)}, device_id_type=MESH
        )
        return carry

    lax.fori_loop(1, experts, greet, 0)
    for to in (ahead, behind):
        pl.semaphore_signal(barrier, inc=1, device_id={"dp": to}, device_id_type=MESH)
    for load in small:
        load.wait()

    expert_of = iota((experts, toks), 0)
    named = jnp.zeros((experts, toks), F32)
    picked = jnp.zeros((experts, toks), F32)
    for k in range(top):
        same = ids_ref[k : k + 1, :] == expert_of
        named = named + jnp.where(same, 1.0, 0.0)
        picked = picked + jnp.where(same, gw_ref[k : k + 1, :], 0.0)
    before = jnp.where(iota((toks, toks), 0) < iota((toks, toks), 1), 1.0, 0.0).astype(BF16)
    earlier = jnp.dot(named.astype(BF16), before, preferred_element_type=F32)
    code = jnp.where(named > 0.0, earlier, -1.0)
    code_ref[...] = code

    pl.semaphore_wait(barrier, experts - 1 + 2)

    def at_distance(i):
        k = mid - quotient(i + 1, 2)
        odd = residue(i, 2)
        return residue(y + odd * k + (1 - odd) * (n - k), n)

    def send_rows(p, h):
        to_z = residue(z + n - p, n)
        for j in range(half):
            dx, dc = divmod(h * half + j, 2)
            to_r = residue(x + n_x - dx, n_x) * 2 + residue(c + dc, 2)
            src, dst = packed.at[to_z, to_r], rows.at[p * 2 + h, j]
            sem = pack_recv.at[p * 2 + h]

            def remote():
                pltpu.make_async_remote_copy(
                    src_ref=src, dst_ref=dst, send_sem=pack_send, recv_sem=sem,
                    device_id={"expert": to_z * per + to_r}, device_id_type=MESH,
                ).start()

            if h == 0 and j == 0:
                pl.when(p != 0)(remote)

                @pl.when(p == 0)
                def _():
                    pltpu.make_async_copy(src, dst, sem).start()

            else:
                remote()

    def pack(i, carry):
        p = at_distance(i)
        to_z = residue(z + n - p, n)
        codes = code_ref[pl.ds(pl.multiple_of(to_z * per, per), per), :]
        slot = iota((per, cap, toks), 1).astype(F32)
        chosen = jnp.where(codes[:, None, :] == slot, 1.0, 0.0).reshape(per * cap, toks)
        block = jnp.dot(chosen.astype(BF16), tok_ref[...], preferred_element_type=F32)
        packed[to_z] = block.astype(BF16).reshape(per, cap, width)
        send_rows(p, 0)
        return carry

    lax.fori_loop(0, n, pack, 0)

    def pack_rest(i, carry):
        send_rows(at_distance(i), 1)
        return carry

    lax.fori_loop(0, n, pack_rest, 0)

    lane = iota((experts, experts * cap), 1)
    spread = jnp.where(lane // cap == iota((experts, experts * cap), 0), 1.0, 0.0).astype(BF16)
    slot_at = jnp.dot(code.T.astype(BF16), spread, preferred_element_type=F32)
    here = slot_at == (iota((toks, experts * cap), 1) % cap).astype(F32)
    weights = picked.T
    high = weights.astype(BF16)
    low = (weights - high.astype(F32)).astype(BF16)
    for k, piece in enumerate((high, low)):
        laid = jnp.dot(piece, spread, preferred_element_type=F32)
        mix_ref[k * toks : (k + 1) * toks, :] = jnp.where(here, laid, 0.0).astype(BF16)

    for load in loads:
        load.wait()

    def await_rows(p, h):
        k = p * 2 + h
        pltpu.make_async_copy(rows.at[k], rows.at[k], pack_recv.at[k]).wait()

    def rows_of(p, h):
        return rows[p * 2 + h].reshape(m_rows, width)

    def reduce_step(h, i, joins):
        k = mid - quotient(i + 1, 2)
        if isinstance(i, int):
            await_rows(residue(y + k, n), h)
            if i:
                await_rows(residue(y + n - k, n), h)
        else:

            @pl.when(residue(i, 2) == 1)
            def _():
                await_rows(residue(y + k, n), h)
                await_rows(residue(y + n - k, n), h)

        for d in (0, 1):
            p = residue(y + (n - k if d else k), n)
            kind = residue(i + d, 2)
            own = rows_of(p, h)
            slot = h * steps + i
            if joins:
                pltpu.make_async_copy(
                    rs_in.at[d, slot - 2], rs_in.at[d, slot - 2], rs_recv.at[d, slot - 2]
                ).wait()
            for f in range(0, ff, tile):
                part = jnp.dot(own, w_buf[kind, :, f : f + tile], preferred_element_type=F32)
                if joins:
                    part = part + rs_in[d, slot - 2, :, f : f + tile].astype(F32)
                rs_out[d, slot, :, f : f + tile] = part.astype(BF16)
            pltpu.make_async_remote_copy(
                src_ref=rs_out.at[d, slot], dst_ref=rs_in.at[d, slot],
                send_sem=rs_send, recv_sem=rs_recv.at[d, slot],
                device_id={"dp": behind if d else ahead}, device_id_type=MESH,
            ).start()

    def reduce_half(h):
        for i in range(2):
            reduce_step(h, i, False)

        def body(i, carry):
            reduce_step(h, i, True)
            return carry

        lax.fori_loop(2, steps, body, 0)

    def finish(h):
        await_rows(y, h)
        last = h * steps + steps - 1
        for d in (0, 1):
            for slot in (last - 1, last):
                pltpu.make_async_copy(
                    rs_in.at[d, slot], rs_in.at[d, slot], rs_recv.at[d, slot]
                ).wait()
        own = rows_of(y, h)
        for f in range(0, ff, tile):
            cut = slice(f, f + tile)
            gate = jnp.dot(own, w_buf[0, :, cut], preferred_element_type=F32)
            gate = gate + rs_in[0, last, :, cut].astype(F32) + rs_in[1, last - 1, :, cut].astype(F32)
            up = jnp.dot(own, w_buf[1, :, cut], preferred_element_type=F32)
            up = up + rs_in[0, last - 1, :, cut].astype(F32) + rs_in[1, last, :, cut].astype(F32)
            hid[h * n + y, :, cut] = (gate / (1.0 + jnp.exp(-gate)) * up).astype(BF16)

    def part_of(h, p, s):
        return hid.at[h * n + p, pl.ds(s * sub_rows, sub_rows)]

    def pass_on(h, s, d, sub):
        part = part_of(h, residue(y + (s if d else n - s), n), sub)
        pltpu.make_async_remote_copy(
            src_ref=part, dst_ref=part, send_sem=ag_send, recv_sem=ag_recv.at[d, h, s, sub],
            device_id={"dp": behind if d else ahead}, device_id_type=MESH,
        ).start()

    def arrived(h, s, d, sub):
        part = part_of(h, residue(y + (s + 1 if d else n - s - 1), n), sub)
        pltpu.make_async_copy(part, part, ag_recv.at[d, h, s, sub]).wait()

    def expert_rows_out(h, p):
        k = h * n + p
        done = jnp.dot(hid[k], d_buf[...], preferred_element_type=F32)
        outs[k] = done.astype(BF16).reshape(half, cap, width)
        to_z = residue(z + p, n)
        for j in range(half):
            dx, dc = divmod(h * half + j, 2)
            to = to_z * per + residue(x + dx, n_x) * 2 + residue(c + dc, 2)
            src, dst = outs.at[k, j], ret.at[me]

            def remote():
                pltpu.make_async_remote_copy(
                    src_ref=src, dst_ref=dst, send_sem=ret_send, recv_sem=ret_recv,
                    device_id={"expert": to}, device_id_type=MESH,
                ).start()

            if h == 0 and j == 0:
                pl.when(p != 0)(remote)

                @pl.when(p == 0)
                def _():
                    pltpu.make_async_copy(src, dst, ret_recv).start()

            else:
                remote()

    def exchange(h, s):
        if s == 0:
            finish(h)
        for sub in (0, 1):
            for d in (0, 1):
                if 0 < s < mid or (s == mid and sub == d):
                    arrived(h, s - 1, d, sub)
                if s < mid - 1 or (s == mid - 1 and sub == d):
                    pass_on(h, s, d, sub)

    def outward(h, s):
        expert_rows_out(h, residue(y + s, n))
        if 0 < s < mid:
            expert_rows_out(h, residue(y + n - s, n))

    reduce_half(0)
    reduce_half(1)
    order = [(0, 0)]
    for s in range(1, mid + 1):
        order += [(0, s), (1, s - 1)]
    order.append((1, mid))
    late = None
    for event in order:
        exchange(*event)
        if late is not None:
            outward(*late)
        late = event
    outward(*late)

    pltpu.make_async_copy(ret, ret, ret_recv).wait()
    back = ret[...].reshape(experts * cap, width)
    mixed = jnp.dot(mix_ref[...], back, preferred_element_type=F32)
    out_ref[...] = (mixed[:toks] + mixed[toks:]).astype(BF16)

    flat = packed.at[0, pl.ds(0, per - 1)]
    pltpu.make_async_copy(flat, flat, pack_send).wait()
    whole = packed.at[pl.ds(0, n - 1)]
    pltpu.make_async_copy(whole, whole, pack_send).wait()
    pltpu.make_async_copy(rs_out, rs_out, rs_send).wait()
    sent = hid.at[pl.ds(0, 2 * n - 2)]
    pltpu.make_async_copy(sent, sent, ag_send).wait()
    back_sent = ret.at[pl.ds(0, experts - 1)]
    pltpu.make_async_copy(back_sent, back_sent, ret_send).wait()


def body(tokens, expert_ids, gate_weights, gate_proj, up_proj, down_proj):
    n, experts = lax.axis_size("dp"), lax.axis_size("expert")
    per = experts // n
    toks, width = tokens.shape
    top = expert_ids.shape[1]
    cap = 2 * toks * top // experts
    ff = gate_proj.shape[2]
    half = per // 2
    m_rows = half * cap
    vmem = pl.BlockSpec(memory_space=pltpu.VMEM)
    hbm = pl.BlockSpec(memory_space=pltpu.HBM)
    flops = 2 * experts * cap * width * ff * 3
    return pl.pallas_call(
        functools.partial(layer, n, per),
        out_shape=jax.ShapeDtypeStruct((toks, width), BF16),
        in_specs=[hbm] * 6,
        out_specs=vmem,
        scratch_shapes=[
            pltpu.VMEM((top, toks), jnp.int32),
            pltpu.VMEM((top, toks), F32),
            pltpu.VMEM((toks, width), BF16),
            pltpu.VMEM((2, width, ff), BF16),
            pltpu.VMEM((ff, width), BF16),
            pltpu.VMEM((experts, toks), F32),
            pltpu.VMEM((2 * toks, experts * cap), BF16),
            pltpu.VMEM((n, per, cap, width), BF16),
            pltpu.VMEM((2 * n, half, cap, width), BF16),
            pltpu.VMEM((2, 2 * (n - 1), m_rows, ff), BF16),
            pltpu.VMEM((2, 2 * (n - 1), m_rows, ff), BF16),
            pltpu.VMEM((2 * n, m_rows, ff), BF16),
            pltpu.VMEM((2 * n, half, cap, width), BF16),
            pltpu.VMEM((experts, cap, width), BF16),
            pltpu.SemaphoreType.DMA((6,)),
            pltpu.SemaphoreType.DMA,
            pltpu.SemaphoreType.DMA((2 * n,)),
            pltpu.SemaphoreType.DMA,
            pltpu.SemaphoreType.DMA((2, 2 * (n - 1))),
            pltpu.SemaphoreType.DMA,
            pltpu.SemaphoreType.DMA((2, 2, n // 2, 2)),
            pltpu.SemaphoreType.DMA,
            pltpu.SemaphoreType.DMA,
        ],
        cost_estimate=pl.CostEstimate(
            flops=flops, bytes_accessed=3 * width * ff * 2, transcendentals=m_rows * 2 * ff
        ),
        compiler_params=pltpu.CompilerParams(
            collective_id=0, has_side_effects=True, vmem_limit_bytes=50 * 2**20
        ),
    )(
        *(
            pltpu.with_memory_space_constraint(a, pltpu.HBM)
            for a in (
                expert_ids.T, gate_weights.T, tokens, gate_proj[0], up_proj[0], down_proj[0]
            )
        )
    )


def solution(mesh):
    placed = (
        P("expert", "dp"),
        P("expert", None),
        P("expert", None),
        P("expert", "dp", None),
        P("expert", "dp", None),
        P("expert", None, "dp"),
    )
    return jax.shard_map(
        body, mesh=mesh, in_specs=placed, out_specs=P("expert", "dp"), check_vma=False
    )
```

time: 267 us -> 133 us (0.50)
  the two profiles are of different devices: /device:TPU:1 before, /device:TPU:57 now
where the time goes in v1:
time: 133 us
  Pallas kernels  132 us (99%)
    pallas_call x1, Pallas kernels, body(): pl.pallas_call(functools.partial(layer, n, per), out_shape=jax.ShapeDtype...  132 us

profile of v1, /device:TPU:57, one launch (start us, length us, event | category | flops | bytes accessed | tf_op | source)
XLA Modules:
  0.0 132.7 jit_solution(13650230399642804716)
XLA Ops:
  0.0 132.1 %shard_map.64 = bf16[64,512]{1,0:T(8,128)(2,1)S(1)} custom-call(s32[8,64]{1,0:T(8,128)} %bitcast.8, f32[8,64]{1,0:T(8,128)} %bitcast.9, bf16[64,512]{1,0:T(8,128)(2,1)} %tok_hbm.1, bf16[512,1536]{1,0:T(8,128)(2,1)} %bitcast.5, bf16[512,1536]{1,0:T(8,128)(2,1)} %bitcast.6, bf16[1536,512]{1,0:T(8,128)(2,1)} %bitcast.7), custom_call_target="tpu_custom_call" | custom-call | flops 4831838208 | bytes 4718592 | tf_op jit(solution)/shard_map/pallas_call | solution.py:314
  132.1 0.6 copy.8

commit v2 on v1

--- a/solution.py
+++ b/solution.py
@@ -18,6 +18,13 @@
 
 def residue(a, b):
     return a % b if isinstance(a, int) else lax.rem(a, jnp.int32(b))
+
+
+def z_shifts(n):
+    near = sorted(range(n), key=lambda k: -min(k, n - k))
+    far = [k for k in near if k != n // 2 and k]
+    order = [0, n // 2] + far
+    return order[: n // 2], order[n // 2 :]
 
 
 def iota(shape, dim):
@@ -42,6 +49,7 @@
     ff = w_buf.shape[2]
     tile = min(ff, 512)
     sub_rows = m_rows // 2
+    shifts = z_shifts(n)
     ahead, behind = residue(y + 1, n), residue(y + n - 1, n)
     steps = n - 1
 
@@ -55,7 +63,7 @@
         pltpu.make_async_copy(up_hbm, w_buf.at[1], load_sem.at[1]),
         pltpu.make_async_copy(down_hbm, d_buf, load_sem.at[2]),
     ]
-    for load in small + loads:
+    for load in small:
         load.start()
     barrier = pltpu.get_barrier_semaphore()
 
@@ -68,10 +76,13 @@
     lax.fori_loop(1, experts, greet, 0)
     for to in (ahead, behind):
         pl.semaphore_signal(barrier, inc=1, device_id={"dp": to}, device_id_type=MESH)
+    for load in loads:
+        load.start()
     for load in small:
         load.wait()
 
-    expert_of = iota((experts, toks), 0)
+    row = iota((experts, toks), 0)
+    expert_of = row % n * per + row // n
     named = jnp.zeros((experts, toks), F32)
     picked = jnp.zeros((experts, toks), F32)
     for k in range(top):
@@ -90,12 +101,17 @@
         odd = residue(i, 2)
         return residue(y + odd * k + (1 - odd) * (n - k), n)
 
+    def taker_of(p):
+        return residue(x + n_x - quotient(p, 2), n_x) * 2 + residue(c + p, 2)
+
+    def giver_of(p):
+        return residue(x + quotient(p, 2), n_x) * 2 + residue(c + p, 2)
+
     def send_rows(p, h):
-        to_z = residue(z + n - p, n)
-        for j in range(half):
-            dx, dc = divmod(h * half + j, 2)
-            to_r = residue(x + n_x - dx, n_x) * 2 + residue(c + dc, 2)
-            src, dst = packed.at[to_z, to_r], rows.at[p * 2 + h, j]
+        to_r = taker_of(p)
+        for j, shift in enumerate(shifts[h]):
+            to_z = residue(z + n - shift, n)
+            src, dst = packed.at[to_r, to_z], rows.at[p * 2 + h, j]
             sem = pack_recv.at[p * 2 + h]
 
             def remote():
@@ -104,7 +120,7 @@
                     device_id={"expert": to_z * per + to_r}, device_id_type=MESH,
                 ).start()
 
-            if h == 0 and j == 0:
+            if shift == 0:
                 pl.when(p != 0)(remote)
 
                 @pl.when(p == 0)
@@ -116,33 +132,16 @@
 
     def pack(i, carry):
         p = at_distance(i)
-        to_z = residue(z + n - p, n)
-        codes = code_ref[pl.ds(pl.multiple_of(to_z * per, per), per), :]
-        slot = iota((per, cap, toks), 1).astype(F32)
-        chosen = jnp.where(codes[:, None, :] == slot, 1.0, 0.0).reshape(per * cap, toks)
+        to_r = taker_of(p)
+        codes = code_ref[pl.ds(pl.multiple_of(to_r * n, n), n), :]
+        slot = iota((n, cap, toks), 1).astype(F32)
+        chosen = jnp.where(codes[:, None, :] == slot, 1.0, 0.0).reshape(n * cap, toks)
         block = jnp.dot(chosen.astype(BF16), tok_ref[...], preferred_element_type=F32)
-        packed[to_z] = block.astype(BF16).reshape(per, cap, width)
+        packed[to_r] = block.astype(BF16).reshape(n, cap, width)
         send_rows(p, 0)
         return carry
 
     lax.fori_loop(0, n, pack, 0)
-
-    def pack_rest(i, carry):
-        send_rows(at_distance(i), 1)
-        return carry
-
-    lax.fori_loop(0, n, pack_rest, 0)
-
-    lane = iota((experts, experts * cap), 1)
-    spread = jnp.where(lane // cap == iota((experts, experts * cap), 0), 1.0, 0.0).astype(BF16)
-    slot_at = jnp.dot(code.T.astype(BF16), spread, preferred_element_type=F32)
-    here = slot_at == (iota((toks, experts * cap), 1) % cap).astype(F32)
-    weights = picked.T
-    high = weights.astype(BF16)
-    low = (weights - high.astype(F32)).astype(BF16)
-    for k, piece in enumerate((high, low)):
-        laid = jnp.dot(piece, spread, preferred_element_type=F32)
-        mix_ref[k * toks : (k + 1) * toks, :] = jnp.where(here, laid, 0.0).astype(BF16)
 
     for load in loads:
         load.wait()
@@ -187,12 +186,32 @@
                 device_id={"dp": behind if d else ahead}, device_id_type=MESH,
             ).start()
 
+    def pack_rest(i, carry):
+        send_rows(at_distance(i), 1)
+        return carry
+
+    def make_mix():
+        lane = iota((experts, experts * cap), 1)
+        spread = jnp.where(lane // cap == iota((experts, experts * cap), 0), 1.0, 0.0).astype(BF16)
+        slot_at = jnp.dot(code_ref[...].T.astype(BF16), spread, preferred_element_type=F32)
+        here = slot_at == (iota((toks, experts * cap), 1) % cap).astype(F32)
+        weights = picked.T
+        high = weights.astype(BF16)
+        low = (weights - high.astype(F32)).astype(BF16)
+        for k, piece in enumerate((high, low)):
+            laid = jnp.dot(piece, spread, preferred_element_type=F32)
+            mix_ref[k * toks : (k + 1) * toks, :] = jnp.where(here, laid, 0.0).astype(BF16)
+
     def reduce_half(h):
         for i in range(2):
             reduce_step(h, i, False)
+        if h == 0:
+            lax.fori_loop(0, n, pack_rest, 0)
 
         def body(i, carry):
             reduce_step(h, i, True)
+            if h == 1:
+                pl.when(i == (steps + 1) // 2)(begin_gather)
             return carry
 
         lax.fori_loop(2, steps, body, 0)
@@ -214,73 +233,93 @@
             up = up + rs_in[0, last - 1, :, cut].astype(F32) + rs_in[1, last, :, cut].astype(F32)
             hid[h * n + y, :, cut] = (gate / (1.0 + jnp.exp(-gate)) * up).astype(BF16)
 
-    def part_of(h, p, s):
-        return hid.at[h * n + p, pl.ds(s * sub_rows, sub_rows)]
-
-    def pass_on(h, s, d, sub):
-        part = part_of(h, residue(y + (s if d else n - s), n), sub)
+    def part_of(u, p, s, d):
+        h, sub = divmod(u, 2)
+        if s < mid - 1:
+            return hid.at[h * n + p, pl.ds(sub * sub_rows, sub_rows)]
+        few = sub_rows // 2
+        return hid.at[h * n + p, pl.ds(sub * sub_rows + d * few, few)]
+
+    def pass_on(u, s, d):
+        part = part_of(u, residue(y + (s if d else n - s), n), s, d)
         pltpu.make_async_remote_copy(
-            src_ref=part, dst_ref=part, send_sem=ag_send, recv_sem=ag_recv.at[d, h, s, sub],
+            src_ref=part, dst_ref=part, send_sem=ag_send, recv_sem=ag_recv.at[d, u, s],
             device_id={"dp": behind if d else ahead}, device_id_type=MESH,
         ).start()
 
-    def arrived(h, s, d, sub):
-        part = part_of(h, residue(y + (s + 1 if d else n - s - 1), n), sub)
-        pltpu.make_async_copy(part, part, ag_recv.at[d, h, s, sub]).wait()
-
-    def expert_rows_out(h, p):
-        k = h * n + p
-        done = jnp.dot(hid[k], d_buf[...], preferred_element_type=F32)
-        outs[k] = done.astype(BF16).reshape(half, cap, width)
-        to_z = residue(z + p, n)
-        for j in range(half):
-            dx, dc = divmod(h * half + j, 2)
-            to = to_z * per + residue(x + dx, n_x) * 2 + residue(c + dc, 2)
-            src, dst = outs.at[k, j], ret.at[me]
-
-            def remote():
-                pltpu.make_async_remote_copy(
-                    src_ref=src, dst_ref=dst, send_sem=ret_send, recv_sem=ret_recv,
-                    device_id={"expert": to}, device_id_type=MESH,
-                ).start()
-
-            if h == 0 and j == 0:
-                pl.when(p != 0)(remote)
-
-                @pl.when(p == 0)
-                def _():
-                    pltpu.make_async_copy(src, dst, ret_recv).start()
-
-            else:
-                remote()
-
-    def exchange(h, s):
-        if s == 0:
-            finish(h)
-        for sub in (0, 1):
-            for d in (0, 1):
-                if 0 < s < mid or (s == mid and sub == d):
-                    arrived(h, s - 1, d, sub)
-                if s < mid - 1 or (s == mid - 1 and sub == d):
-                    pass_on(h, s, d, sub)
-
-    def outward(h, s):
-        expert_rows_out(h, residue(y + s, n))
+    def arrived(u, s, d):
+        part = part_of(u, residue(y + (s + 1 if d else n - s - 1), n), s, d)
+        pltpu.make_async_copy(part, part, ag_recv.at[d, u, s]).wait()
+
+    def exchange(u, s):
+        for d in (0, 1):
+            if s > 0:
+                arrived(u, s - 1, d)
+            if s < mid:
+                pass_on(u, s, d)
+
+    def outward(u, s):
+        h, sub = divmod(u, 2)
+        pieces = [residue(y + s, n)]
         if 0 < s < mid:
-            expert_rows_out(h, residue(y + n - s, n))
+            pieces.append(residue(y + n - s, n))
+        keys = [h * n + p for p in pieces]
+        cut = slice(sub * sub_rows, (sub + 1) * sub_rows)
+        held = jnp.concatenate([hid[k, cut] for k in keys], axis=0)
+        done = jnp.dot(held, d_buf[...], preferred_element_type=F32).astype(BF16)
+        some = half // 2
+        for i, (k, p) in enumerate(zip(keys, pieces)):
+            block = done[i * sub_rows : (i + 1) * sub_rows]
+            outs[k, sub * some : (sub + 1) * some] = block.reshape(some, cap, width)
+            to_r = giver_of(p)
+            for j in range(sub * some, (sub + 1) * some):
+                shift = shifts[h][j]
+                src, dst = outs.at[k, j], ret.at[r * n + z]
+                to = residue(z + shift, n) * per + to_r
+
+                def remote():
+                    pltpu.make_async_remote_copy(
+                        src_ref=src, dst_ref=dst, send_sem=ret_send, recv_sem=ret_recv,
+                        device_id={"expert": to}, device_id_type=MESH,
+                    ).start()
+
+                if shift == 0:
+                    pl.when(p != 0)(remote)
+
+                    @pl.when(p == 0)
+                    def _():
+                        pltpu.make_async_copy(src, dst, ret_recv).start()
+
+                else:
+                    remote()
+
+    def begin_gather():
+        finish(0)
+        for u in (0, 1):
+            exchange(u, 0)
+        for u in (0, 1):
+            outward(u, 0)
 
     reduce_half(0)
+    make_mix()
     reduce_half(1)
-    order = [(0, 0)]
-    for s in range(1, mid + 1):
-        order += [(0, s), (1, s - 1)]
-    order.append((1, mid))
+    order = [
+        (0, 1), (1, 1), (0, 2), (2, 0), (1, 2), (0, 3), (3, 0), (1, 3), (0, 4), (2, 1),
+        (1, 4), (3, 1), (2, 2), (3, 2), (2, 3), (3, 3), (2, 4), (3, 4),
+    ]
     late = None
-    for event in order:
-        exchange(*event)
-        if late is not None:
+    for u, s in order:
+        if s > mid:
+            continue
+        if s == mid and late:
             outward(*late)
-        late = event
+            late = None
+        if (u, s) == (2, 0):
+            finish(1)
+        exchange(u, s)
+        if late:
+            outward(*late)
+        late = (u, s)
     outward(*late)
 
     pltpu.make_async_copy(ret, ret, ret_recv).wait()
@@ -302,6 +341,7 @@
 def body(tokens, expert_ids, gate_weights, gate_proj, up_proj, down_proj):
     n, experts = lax.axis_size("dp"), lax.axis_size("expert")
     per = experts // n
+    assert per == n
     toks, width = tokens.shape
     top = expert_ids.shape[1]
     cap = 2 * toks * top // experts
@@ -337,7 +377,7 @@
             pltpu.SemaphoreType.DMA,
             pltpu.SemaphoreType.DMA((2, 2 * (n - 1))),
             pltpu.SemaphoreType.DMA,
-            pltpu.SemaphoreType.DMA((2, 2, n // 2, 2)),
+            pltpu.SemaphoreType.DMA((2, 4, n // 2)),
             pltpu.SemaphoreType.DMA,
             pltpu.SemaphoreType.DMA,
         ],

time: 133 us -> 122 us (0.917)
  the two profiles are of different devices: /device:TPU:57 before, /device:TPU:1 now
where the time goes in v2:
time: 122 us
  Pallas kernels  121 us (99%)
    pallas_call x1, Pallas kernels, body(): pl.pallas_call(functools.partial(layer, n, per), out_shape=jax.ShapeDtype...  121 us

profile of v2, /device:TPU:1, one launch (start us, length us, event | category | flops | bytes accessed | tf_op | source)
XLA Modules:
  0.0 122.0 jit_solution(217720932480567863)
XLA Ops:
  0.0 121.4 %shard_map.64 = bf16[64,512]{1,0:T(8,128)(2,1)S(1)} custom-call(s32[8,64]{1,0:T(8,128)} %bitcast.8, f32[8,64]{1,0:T(8,128)} %bitcast.9, bf16[64,512]{1,0:T(8,128)(2,1)} %tok_hbm.1, bf16[512,1536]{1,0:T(8,128)(2,1)} %bitcast.5, bf16[512,1536]{1,0:T(8,128)(2,1)} %bitcast.6, bf16[1536,512]{1,0:T(8,128)(2,1)} %bitcast.7), custom_call_target="tpu_custom_call" | custom-call | flops 4831838208 | bytes 4718592 | tf_op jit(solution)/shard_map/pallas_call | solution.py:354
  121.4 0.6 copy.8

commit v3 on v2

--- a/solution.py
+++ b/solution.py
@@ -21,10 +21,9 @@
 
 
 def z_shifts(n):
-    near = sorted(range(n), key=lambda k: -min(k, n - k))
-    far = [k for k in near if k != n // 2 and k]
-    order = [0, n // 2] + far
-    return order[: n // 2], order[n // 2 :]
+    order = sorted(range(n), key=lambda k: min(k, n - k))
+    near, far = order[: n // 2], order[n // 2 :]
+    return near[:1] + near[-1:] + near[1:-1], far[-1:] + far[:-1]
 
 
 def iota(shape, dim):
@@ -63,7 +62,7 @@
         pltpu.make_async_copy(up_hbm, w_buf.at[1], load_sem.at[1]),
         pltpu.make_async_copy(down_hbm, d_buf, load_sem.at[2]),
     ]
-    for load in small:
+    for load in small + loads:
         load.start()
     barrier = pltpu.get_barrier_semaphore()
 
@@ -76,8 +75,6 @@
     lax.fori_loop(1, experts, greet, 0)
     for to in (ahead, behind):
         pl.semaphore_signal(barrier, inc=1, device_id={"dp": to}, device_id_type=MESH)
-    for load in loads:
-        load.start()
     for load in small:
         load.wait()
 
@@ -141,9 +138,8 @@
         send_rows(p, 0)
         return carry
 
-    lax.fori_loop(0, n, pack, 0)
-
-    for load in loads:
+    lax.fori_loop(0, n // 2, pack, 0)
+    for load in loads[:2]:
         load.wait()
 
     def await_rows(p, h):
@@ -205,8 +201,11 @@
     def reduce_half(h):
         for i in range(2):
             reduce_step(h, i, False)
+            if (h, i) == (0, 0):
+                lax.fori_loop(n // 2, n, pack, 0)
         if h == 0:
             lax.fori_loop(0, n, pack_rest, 0)
+            loads[2].wait()
 
         def body(i, carry):
             reduce_step(h, i, True)
@@ -295,17 +294,15 @@
 
     def begin_gather():
         finish(0)
-        for u in (0, 1):
-            exchange(u, 0)
-        for u in (0, 1):
-            outward(u, 0)
+        exchange(0, 0)
+        outward(0, 0)
 
     reduce_half(0)
     make_mix()
     reduce_half(1)
     order = [
-        (0, 1), (1, 1), (0, 2), (2, 0), (1, 2), (0, 3), (3, 0), (1, 3), (0, 4), (2, 1),
-        (1, 4), (3, 1), (2, 2), (3, 2), (2, 3), (3, 3), (2, 4), (3, 4),
+        (0, 1), (1, 0), (2, 0), (0, 2), (3, 0), (2, 1), (0, 3), (3, 1), (2, 2), (0, 4),
+        (1, 1), (3, 2), (2, 3), (1, 2), (3, 3), (2, 4), (1, 3), (3, 4), (1, 4),
     ]
     late = None
     for u, s in order:

time: 122 us -> 120 us (0.984)
    pallas_call x1, Pallas kernels: 121 us -> 120 us  [body(): pl.pallas_call(functools.partial(layer, n, per), out_shape=jax.ShapeDtype...]
where the time goes in v3:
time: 120 us
  Pallas kernels  120 us (100%)
    pallas_call x1, Pallas kernels, body(): pl.pallas_call(functools.partial(layer, n, per), out_shape=jax.ShapeDtype...  120 us

profile of v3, /device:TPU:1, one launch (start us, length us, event | category | flops | bytes accessed | tf_op | source)
XLA Modules:
  0.0 120.3 jit_solution(5382175006912522058)
XLA Ops:
  0.0 119.7 %shard_map.64 = bf16[64,512]{1,0:T(8,128)(2,1)S(1)} custom-call(s32[8,64]{1,0:T(8,128)} %bitcast.8, f32[8,64]{1,0:T(8,128)} %bitcast.9, bf16[64,512]{1,0:T(8,128)(2,1)} %tok_hbm.1, bf16[512,1536]{1,0:T(8,128)(2,1)} %bitcast.5, bf16[512,1536]{1,0:T(8,128)(2,1)} %bitcast.6, bf16[1536,512]{1,0:T(8,128)(2,1)} %bitcast.7), custom_call_target="tpu_custom_call" | custom-call | flops 4831838208 | bytes 4718592 | tf_op jit(solution)/shard_map/pallas_call | solution.py:351
  119.7 0.6 copy.8

commit v4 on v3

--- a/solution.py
+++ b/solution.py
@@ -32,7 +32,7 @@
 
 def layer(
     n, per, ids_hbm, gw_hbm, tok_hbm, gate_hbm, up_hbm, down_hbm, out_ref,
-    ids_ref, gw_ref, tok_ref, w_buf, d_buf, code_ref, mix_ref, packed, rows, rs_out, rs_in, hid, outs, ret,
+    ids_ref, gw_ref, tok_ref, w_buf, d_buf, code_ref, mix_ref, packed, rows, parts, rs_out, rs_in, hid, outs, ret,
     load_sem, pack_send, pack_recv, rs_send, rs_recv, ag_send, ag_recv, ret_send, ret_recv,
 ):
     y = lax.axis_index("dp")
@@ -149,6 +149,13 @@
     def rows_of(p, h):
         return rows[p * 2 + h].reshape(m_rows, width)
 
+    def send_sums(d, slot):
+        pltpu.make_async_remote_copy(
+            src_ref=rs_out.at[d, slot], dst_ref=rs_in.at[d, slot],
+            send_sem=rs_send, recv_sem=rs_recv.at[d, slot],
+            device_id={"dp": behind if d else ahead}, device_id_type=MESH,
+        ).start()
+
     def reduce_step(h, i, joins):
         k = mid - quotient(i + 1, 2)
         if isinstance(i, int):
@@ -162,25 +169,25 @@
                 await_rows(residue(y + k, n), h)
                 await_rows(residue(y + n - k, n), h)
 
+        slot = h * steps + i
         for d in (0, 1):
-            p = residue(y + (n - k if d else k), n)
+            own = rows_of(residue(y + (n - k if d else k), n), h)
             kind = residue(i + d, 2)
-            own = rows_of(p, h)
-            slot = h * steps + i
-            if joins:
-                pltpu.make_async_copy(
-                    rs_in.at[d, slot - 2], rs_in.at[d, slot - 2], rs_recv.at[d, slot - 2]
-                ).wait()
             for f in range(0, ff, tile):
-                part = jnp.dot(own, w_buf[kind, :, f : f + tile], preferred_element_type=F32)
+                cut = slice(f, f + tile)
+                part = jnp.dot(own, w_buf[kind, :, cut], preferred_element_type=F32)
                 if joins:
-                    part = part + rs_in[d, slot - 2, :, f : f + tile].astype(F32)
-                rs_out[d, slot, :, f : f + tile] = part.astype(BF16)
-            pltpu.make_async_remote_copy(
-                src_ref=rs_out.at[d, slot], dst_ref=rs_in.at[d, slot],
-                send_sem=rs_send, recv_sem=rs_recv.at[d, slot],
-                device_id={"dp": behind if d else ahead}, device_id_type=MESH,
-            ).start()
+                    parts[d, :, cut] = part
+                else:
+                    rs_out[d, slot, :, cut] = part.astype(BF16)
+            if not joins:
+                send_sums(d, slot)
+        if joins:
+            for d in (0, 1):
+                came = rs_in.at[d, slot - 2]
+                pltpu.make_async_copy(came, came, rs_recv.at[d, slot - 2]).wait()
+                rs_out[d, slot] = (parts[d] + came[...].astype(F32)).astype(BF16)
+                send_sums(d, slot)
 
     def pack_rest(i, carry):
         send_rows(at_distance(i), 1)
@@ -204,12 +211,18 @@
             if (h, i) == (0, 0):
                 lax.fori_loop(n // 2, n, pack, 0)
         if h == 0:
-            lax.fori_loop(0, n, pack_rest, 0)
+            lax.fori_loop(0, n // 2, pack_rest, 0)
             loads[2].wait()
 
         def body(i, carry):
             reduce_step(h, i, True)
-            if h == 1:
+            if h == 0:
+
+                @pl.when(i == 2)
+                def _():
+                    lax.fori_loop(n // 2, n, pack_rest, 0)
+
+            else:
                 pl.when(i == (steps + 1) // 2)(begin_gather)
             return carry
 
@@ -217,19 +230,25 @@
 
     def finish(h):
         await_rows(y, h)
+        own = rows_of(y, h)
+        for kind in (0, 1):
+            for f in range(0, ff, tile):
+                cut = slice(f, f + tile)
+                parts[kind, :, cut] = jnp.dot(
+                    own, w_buf[kind, :, cut], preferred_element_type=F32
+                )
         last = h * steps + steps - 1
         for d in (0, 1):
             for slot in (last - 1, last):
                 pltpu.make_async_copy(
                     rs_in.at[d, slot], rs_in.at[d, slot], rs_recv.at[d, slot]
                 ).wait()
-        own = rows_of(y, h)
         for f in range(0, ff, tile):
             cut = slice(f, f + tile)
-            gate = jnp.dot(own, w_buf[0, :, cut], preferred_element_type=F32)
-            gate = gate + rs_in[0, last, :, cut].astype(F32) + rs_in[1, last - 1, :, cut].astype(F32)
-            up = jnp.dot(own, w_buf[1, :, cut], preferred_element_type=F32)
-            up = up + rs_in[0, last - 1, :, cut].astype(F32) + rs_in[1, last, :, cut].astype(F32)
+            gate = parts[0, :, cut] + rs_in[0, last, :, cut].astype(F32)
+            gate = gate + rs_in[1, last - 1, :, cut].astype(F32)
+            up = parts[1, :, cut] + rs_in[0, last - 1, :, cut].astype(F32)
+            up = up + rs_in[1, last, :, cut].astype(F32)
             hid[h * n + y, :, cut] = (gate / (1.0 + jnp.exp(-gate)) * up).astype(BF16)
 
     def part_of(u, p, s, d):
@@ -363,6 +382,7 @@
             pltpu.VMEM((2 * toks, experts * cap), BF16),
             pltpu.VMEM((n, per, cap, width), BF16),
             pltpu.VMEM((2 * n, half, cap, width), BF16),
+            pltpu.VMEM((2, m_rows, ff), F32),
             pltpu.VMEM((2, 2 * (n - 1), m_rows, ff), BF16),
             pltpu.VMEM((2, 2 * (n - 1), m_rows, ff), BF16),
             pltpu.VMEM((2 * n, m_rows, ff), BF16),

time: 120 us -> 120 us (level)
  no operation moved by 1% of the time
where the time goes in v4:
time: 120 us
  Pallas kernels  120 us (100%)
    pallas_call x1, Pallas kernels, body(): pl.pallas_call(functools.partial(layer, n, per), out_shape=jax.ShapeDtype...  120 us

profile of v4, /device:TPU:1, one launch (start us, length us, event | category | flops | bytes accessed | tf_op | source)
XLA Modules:
  0.0 120.3 jit_solution(4927273837413152960)
XLA Ops:
  0.0 119.7 %shard_map.64 = bf16[64,512]{1,0:T(8,128)(2,1)S(1)} custom-call(s32[8,64]{1,0:T(8,128)} %bitcast.8, f32[8,64]{1,0:T(8,128)} %bitcast.9, bf16[64,512]{1,0:T(8,128)(2,1)} %tok_hbm.1, bf16[512,1536]{1,0:T(8,128)(2,1)} %bitcast.5, bf16[512,1536]{1,0:T(8,128)(2,1)} %bitcast.6, bf16[1536,512]{1,0:T(8,128)(2,1)} %bitcast.7), custom_call_target="tpu_custom_call" | custom-call | flops 4831838208 | bytes 4718592 | tf_op jit(solution)/shard_map/pallas_call | solution.py:370
  119.7 0.6 copy.8

commit v5 on v4

--- a/solution.py
+++ b/solution.py
@@ -98,18 +98,30 @@
         odd = residue(i, 2)
         return residue(y + odd * k + (1 - odd) * (n - k), n)
 
-    def taker_of(p):
-        return residue(x + n_x - quotient(p, 2), n_x) * 2 + residue(c + p, 2)
-
-    def giver_of(p):
-        return residue(x + quotient(p, 2), n_x) * 2 + residue(c + p, 2)
-
-    def send_rows(p, h):
-        to_r = taker_of(p)
-        for j, shift in enumerate(shifts[h]):
-            to_z = residue(z + n - shift, n)
-            src, dst = packed.at[to_r, to_z], rows.at[p * 2 + h, j]
-            sem = pack_recv.at[p * 2 + h]
+    def taker_of(p, j):
+        dx = residue(quotient(p, 2) + j, n_x)
+        return residue(x + n_x - dx, n_x) * 2 + residue(c + p, 2)
+
+    def giver_of(p, j):
+        dx = residue(quotient(p, 2) + j, n_x)
+        return residue(x + dx, n_x) * 2 + residue(c + p, 2)
+
+    def pack(h, i):
+        p = at_distance(i)
+        key = p * 2 + h
+        takers = [(taker_of(p, j), residue(z + n - shift, n)) for j, shift in enumerate(shifts[h])]
+        slot = iota((cap, toks), 0).astype(F32)
+        chosen = jnp.concatenate(
+            [
+                jnp.where(code_ref[pl.ds(to_r * n + to_z, 1), :] == slot, 1.0, 0.0)
+                for to_r, to_z in takers
+            ],
+            axis=0,
+        )
+        block = jnp.dot(chosen.astype(BF16), tok_ref[...], preferred_element_type=F32)
+        packed[key] = block.astype(BF16).reshape(half, cap, width)
+        for j, (to_r, to_z) in enumerate(takers):
+            src, dst, sem = packed.at[key, j], rows.at[key, j], pack_recv.at[key]
 
             def remote():
                 pltpu.make_async_remote_copy(
@@ -117,7 +129,7 @@
                     device_id={"expert": to_z * per + to_r}, device_id_type=MESH,
                 ).start()
 
-            if shift == 0:
+            if shifts[h][j] == 0:
                 pl.when(p != 0)(remote)
 
                 @pl.when(p == 0)
@@ -127,18 +139,14 @@
             else:
                 remote()
 
-    def pack(i, carry):
-        p = at_distance(i)
-        to_r = taker_of(p)
-        codes = code_ref[pl.ds(pl.multiple_of(to_r * n, n), n), :]
-        slot = iota((n, cap, toks), 1).astype(F32)
-        chosen = jnp.where(codes[:, None, :] == slot, 1.0, 0.0).reshape(n * cap, toks)
-        block = jnp.dot(chosen.astype(BF16), tok_ref[...], preferred_element_type=F32)
-        packed[to_r] = block.astype(BF16).reshape(n, cap, width)
-        send_rows(p, 0)
-        return carry
-
-    lax.fori_loop(0, n // 2, pack, 0)
+    def pack_range(h, start, stop):
+        def one(i, carry):
+            pack(h, i)
+            return carry
+
+        lax.fori_loop(start, stop, one, 0)
+
+    pack_range(0, 0, n // 2)
     for load in loads[:2]:
         load.wait()
 
@@ -189,10 +197,6 @@
                 rs_out[d, slot] = (parts[d] + came[...].astype(F32)).astype(BF16)
                 send_sums(d, slot)
 
-    def pack_rest(i, carry):
-        send_rows(at_distance(i), 1)
-        return carry
-
     def make_mix():
         lane = iota((experts, experts * cap), 1)
         spread = jnp.where(lane // cap == iota((experts, experts * cap), 0), 1.0, 0.0).astype(BF16)
@@ -209,9 +213,9 @@
         for i in range(2):
             reduce_step(h, i, False)
             if (h, i) == (0, 0):
-                lax.fori_loop(n // 2, n, pack, 0)
+                pack_range(0, n // 2, n)
         if h == 0:
-            lax.fori_loop(0, n // 2, pack_rest, 0)
+            pack_range(1, 0, n // 2)
             loads[2].wait()
 
         def body(i, carry):
@@ -220,7 +224,7 @@
 
                 @pl.when(i == 2)
                 def _():
-                    lax.fori_loop(n // 2, n, pack_rest, 0)
+                    pack_range(1, n // 2, n)
 
             else:
                 pl.when(i == (steps + 1) // 2)(begin_gather)
@@ -289,11 +293,10 @@
         for i, (k, p) in enumerate(zip(keys, pieces)):
             block = done[i * sub_rows : (i + 1) * sub_rows]
             outs[k, sub * some : (sub + 1) * some] = block.reshape(some, cap, width)
-            to_r = giver_of(p)
             for j in range(sub * some, (sub + 1) * some):
                 shift = shifts[h][j]
                 src, dst = outs.at[k, j], ret.at[r * n + z]
-                to = residue(z + shift, n) * per + to_r
+                to = residue(z + shift, n) * per + giver_of(p, j)
 
                 def remote():
                     pltpu.make_async_remote_copy(
@@ -343,9 +346,9 @@
     mixed = jnp.dot(mix_ref[...], back, preferred_element_type=F32)
     out_ref[...] = (mixed[:toks] + mixed[toks:]).astype(BF16)
 
-    flat = packed.at[0, pl.ds(0, per - 1)]
+    flat = packed.at[0, pl.ds(0, half - 1)]
     pltpu.make_async_copy(flat, flat, pack_send).wait()
-    whole = packed.at[pl.ds(0, n - 1)]
+    whole = packed.at[pl.ds(0, 2 * n - 1)]
     pltpu.make_async_copy(whole, whole, pack_send).wait()
     pltpu.make_async_copy(rs_out, rs_out, rs_send).wait()
     sent = hid.at[pl.ds(0, 2 * n - 2)]
@@ -380,7 +383,7 @@
             pltpu.VMEM((ff, width), BF16),
             pltpu.VMEM((experts, toks), F32),
             pltpu.VMEM((2 * toks, experts * cap), BF16),
-            pltpu.VMEM((n, per, cap, width), BF16),
+            pltpu.VMEM((2 * n, half, cap, width), BF16),
             pltpu.VMEM((2 * n, half, cap, width), BF16),
             pltpu.VMEM((2, m_rows, ff), F32),
             pltpu.VMEM((2, 2 * (n - 1), m_rows, ff), BF16),

time: 120 us -> 120 us (level)
  no operation moved by 1% of the time
where the time goes in v5:
time: 120 us
  Pallas kernels  119 us (99%)
    pallas_call x1, Pallas kernels, body(): pl.pallas_call(functools.partial(layer, n, per), out_shape=jax.ShapeDtype...  119 us

profile of v5, /device:TPU:1, one launch (start us, length us, event | category | flops | bytes accessed | tf_op | source)
XLA Modules:
  0.0 120.0 jit_solution(17960802572731644206)
XLA Ops:
  0.0 119.4 %shard_map.64 = bf16[64,512]{1,0:T(8,128)(2,1)S(1)} custom-call(s32[8,64]{1,0:T(8,128)} %bitcast.8, f32[8,64]{1,0:T(8,128)} %bitcast.9, bf16[64,512]{1,0:T(8,128)(2,1)} %tok_hbm.1, bf16[512,1536]{1,0:T(8,128)(2,1)} %bitcast.5, bf16[512,1536]{1,0:T(8,128)(2,1)} %bitcast.6, bf16[1536,512]{1,0:T(8,128)(2,1)} %bitcast.7), custom_call_target="tpu_custom_call" | custom-call | flops 4831838208 | bytes 4718592 | tf_op jit(solution)/shard_map/pallas_call | solution.py:373
  119.4 0.6 copy.8

commit v6 on v5

--- a/solution.py
+++ b/solution.py
@@ -323,8 +323,8 @@
     make_mix()
     reduce_half(1)
     order = [
-        (0, 1), (1, 0), (2, 0), (0, 2), (3, 0), (2, 1), (0, 3), (3, 1), (2, 2), (0, 4),
-        (1, 1), (3, 2), (2, 3), (1, 2), (3, 3), (2, 4), (1, 3), (3, 4), (1, 4),
+        (0, 1), (1, 0), (2, 0), (3, 0), (0, 2), (2, 1), (3, 1), (0, 3), (2, 2), (1, 1),
+        (3, 2), (1, 2), (2, 3), (0, 4), (3, 3), (1, 3), (2, 4), (3, 4), (1, 4),
     ]
     late = None
     for u, s in order:

time: 120 us -> 122 us (1.017)
  Pallas kernels: 119 us -> 121 us
    pallas_call x1, Pallas kernels: 119 us -> 121 us  [body(): pl.pallas_call(functools.partial(layer, n, per), out_shape=jax.ShapeDtype...]
where the time goes in v6:
time: 122 us
  Pallas kernels  121 us (99%)
    pallas_call x1, Pallas kernels, body(): pl.pallas_call(functools.partial(layer, n, per), out_shape=jax.ShapeDtype...  121 us

profile of v6, /device:TPU:1, one launch (start us, length us, event | category | flops | bytes accessed | tf_op | source)
XLA Modules:
  0.0 122.1 jit_solution(10209620233446876924)
XLA Ops:
  0.0 121.4 %shard_map.64 = bf16[64,512]{1,0:T(8,128)(2,1)S(1)} custom-call(s32[8,64]{1,0:T(8,128)} %bitcast.8, f32[8,64]{1,0:T(8,128)} %bitcast.9, bf16[64,512]{1,0:T(8,128)(2,1)} %tok_hbm.1, bf16[512,1536]{1,0:T(8,128)(2,1)} %bitcast.5, bf16[512,1536]{1,0:T(8,128)(2,1)} %bitcast.6, bf16[1536,512]{1,0:T(8,128)(2,1)} %bitcast.7), custom_call_target="tpu_custom_call" | custom-call | flops 4831838208 | bytes 4718592 | tf_op jit(solution)/shard_map/pallas_call | solution.py:373
  121.4 0.6 copy.8

commit v7 on v5

--- a/solution.py
+++ b/solution.py
@@ -146,7 +146,7 @@
 
         lax.fori_loop(start, stop, one, 0)
 
-    pack_range(0, 0, n // 2)
+    pack_range(0, 0, n // 2 - 1)
     for load in loads[:2]:
         load.wait()
 
@@ -213,7 +213,7 @@
         for i in range(2):
             reduce_step(h, i, False)
             if (h, i) == (0, 0):
-                pack_range(0, n // 2, n)
+                pack_range(0, n // 2 - 1, n)
         if h == 0:
             pack_range(1, 0, n // 2)
             loads[2].wait()
@@ -324,7 +324,7 @@
     reduce_half(1)
     order = [
         (0, 1), (1, 0), (2, 0), (0, 2), (3, 0), (2, 1), (0, 3), (3, 1), (2, 2), (0, 4),
-        (1, 1), (3, 2), (2, 3), (1, 2), (3, 3), (2, 4), (1, 3), (3, 4), (1, 4),
+        (1, 1), (3, 2), (2, 3), (1, 2), (3, 3), (1, 3), (2, 4), (3, 4), (1, 4),
     ]
     late = None
     for u, s in order:

time: 120 us -> 122 us (1.017)
  Pallas kernels: 119 us -> 121 us
    pallas_call x1, Pallas kernels: 119 us -> 121 us  [body(): pl.pallas_call(functools.partial(layer, n, per), out_shape=jax.ShapeDtype...]
where the time goes in v7:
time: 122 us
  Pallas kernels  121 us (99%)
    pallas_call x1, Pallas kernels, body(): pl.pallas_call(functools.partial(layer, n, per), out_shape=jax.ShapeDtype...  121 us

profile of v7, /device:TPU:1, one launch (start us, length us, event | category | flops | bytes accessed | tf_op | source)
XLA Modules:
  0.0 121.6 jit_solution(4624573830365613358)
XLA Ops:
  0.0 121.0 %shard_map.64 = bf16[64,512]{1,0:T(8,128)(2,1)S(1)} custom-call(s32[8,64]{1,0:T(8,128)} %bitcast.8, f32[8,64]{1,0:T(8,128)} %bitcast.9, bf16[64,512]{1,0:T(8,128)(2,1)} %tok_hbm.1, bf16[512,1536]{1,0:T(8,128)(2,1)} %bitcast.5, bf16[512,1536]{1,0:T(8,128)(2,1)} %bitcast.6, bf16[1536,512]{1,0:T(8,128)(2,1)} %bitcast.7), custom_call_target="tpu_custom_call" | custom-call | flops 4831838208 | bytes 4718592 | tf_op jit(solution)/shard_map/pallas_call | solution.py:373
  121.0 0.6 copy.8
